TPU v7x, 32 devices: a whole 2x2x4 slice. The times are simulated.
32 devices in a mesh: groups: 2 (over y), slab: 16 (over z, x, core).
Axes of the slice: x: 2, y: 2, z: 4, core: 2. Of those that a mesh axis runs over, the one named last changes fastest.
Arguments:
- rhs: float32 [2, 64, 128, 128], P('groups', 'slab'), parts along dimension 0, may hold values from -6 to 6
- labels: int32 [64, 256, 128], P('slab', 'groups'), parts along dimension 1, may hold values from 0 to 4, as said below
- sigma_table: float32 [5, 3], replicated, may hold values from 0.05 to 2
Outputs:
- correction: float32 [2, 64, 128, 128], P('groups', 'slab'), parts along dimension 0
There are 2 independent parts, one for each index of `groups`. A program takes and returns all parts, laid end to end along the dimension named above; an argument that names none is the same for every part. Nothing has to cross between parts.
Inputs may be any that keep to these rules, and one draw needn't show every extreme that they name: Label 0 marks exactly the voxels outside an ellipsoid centred on the grid with semi-axes 0.45 * 128, 0.45 * 128 and 0.55 * 64 cells; inside, labels 1 to 4 are drawn independently for each voxel.
All inputs are finite; a program needn't handle non-finite values.
Results may differ from a plain program's by a relative error of at most 0.0002.
Values sent between devices are 32-bit elements; how exact they have to be, the bound alone decides.
A program may use at most 64 MiB of HBM per device.

v0:
```python
import jax
import jax.numpy as jnp
from jax import lax
from jax.sharding import PartitionSpec as P

LABELS = 5
OMEGA = 0.8


def extended_2(shard, sides, width):
    for axis, dim in sides:
        size, length = (lax.axis_size(axis), shard.shape[dim])
        up = [(i, (i + 1) % size) for i in range(size - 1)]
        down = [(j, i) for i, j in up]
        last = lax.slice_in_dim(shard, length - width, length, axis=dim)
        first = lax.slice_in_dim(shard, 0, width, axis=dim)
        before = lax.ppermute(last, axis, up)
        after = lax.ppermute(first, axis, down)
        shard = jnp.concatenate([before, shard, after], axis=dim)
    return shard


def harmonic(lower_side, upper_side):
    return 2.0 * lower_side * upper_side / (lower_side + upper_side)


def conductivity(padded, sigma_table, column):
    running = jnp.zeros(padded.shape, jnp.float32)
    for tissue in range(LABELS):
        running = running + jnp.where(padded == tissue, sigma_table[tissue, column], 0.0)
    return running


def coefficients(labels_ext, sigma_table):
    padded = jnp.pad(labels_ext, ((0, 0), (1, 1), (1, 1)))
    active = (padded > 0).astype(jnp.float32)
    sigma_x = conductivity(padded, sigma_table, 0)
    sigma_y = conductivity(padded, sigma_table, 1)
    sigma_z = conductivity(padded, sigma_table, 2)
    inner_x = harmonic(sigma_x[1:-1, :-1, 1:-1], sigma_x[1:-1, 1:, 1:-1])
    couple_x = inner_x * active[1:-1, :-1, 1:-1] * active[1:-1, 1:, 1:-1]
    inner_y = harmonic(sigma_y[1:-1, 1:-1, :-1], sigma_y[1:-1, 1:-1, 1:])
    couple_y = inner_y * active[1:-1, 1:-1, :-1] * active[1:-1, 1:-1, 1:]
    inner_z = harmonic(sigma_z[:-1, 1:-1, 1:-1], sigma_z[1:, 1:-1, 1:-1])
    couple_z = inner_z * active[:-1, 1:-1, 1:-1] * active[1:, 1:-1, 1:-1]
    centre_mask = active[1:-1, 1:-1, 1:-1]
    faces = (
        inner_x[:, :-1]
        + inner_x[:, 1:]
        + inner_y[:, :, :-1]
        + inner_y[:, :, 1:]
        + inner_z[:-1]
        + inner_z[1:]
    )
    diagonal = centre_mask * faces + (1.0 - centre_mask)
    return (centre_mask, diagonal, couple_x, couple_y, couple_z)


def operate(extended, terms):
    couple_x, couple_y, couple_z = (terms[2], terms[3], terms[4])
    centre = extended[:, 1:-1]
    widened = jnp.pad(centre, ((0, 0), (0, 0), (1, 1), (1, 1)))
    neighbours = (
        couple_x[:, :-1] * widened[:, :, :-2, 1:-1] + couple_x[:, 1:] * widened[:, :, 2:, 1:-1]
    )
    neighbours = (
        neighbours
        + couple_y[:, :, :-1] * widened[:, :, 1:-1, :-2]
        + couple_y[:, :, 1:] * widened[:, :, 1:-1, 2:]
    )
    neighbours = neighbours + couple_z[:-1] * extended[:, :-2] + couple_z[1:] * extended[:, 2:]
    return terms[1] * centre - neighbours


def smooth(extended, source, terms):
    image = operate(extended, terms)
    return extended[:, 1:-1] + OMEGA * terms[0] * (source - image) / terms[1]


def start(source, terms):
    return OMEGA * terms[0] * source / terms[1]


def leftover(extended, source, terms):
    return terms[0] * (source - operate(extended, terms))


def pair_matrix(length):
    rows_index = lax.broadcasted_iota(jnp.int32, (length, length // 2), 0)
    cols_index = lax.broadcasted_iota(jnp.int32, (length, length // 2), 1)
    return (rows_index // 2 == cols_index).astype(jnp.float32)


def pair_sum(values, along):
    if along == values.ndim - 1:
        return jnp.matmul(values, pair_matrix(values.shape[-1]), precision=lax.Precision.HIGHEST)
    folded = values.shape[:along] + (values.shape[along] // 2, 2) + values.shape[along + 1 :]
    return jnp.sum(values.reshape(folded), axis=along + 1)


def coarsen(terms):
    centre_mask, diagonal, couple_x, couple_y, couple_z = terms
    coarse_x = pair_sum(pair_sum(couple_x[:, 0::2], 0), 2)
    coarse_y = pair_sum(pair_sum(couple_y[:, :, 0::2], 0), 1)
    coarse_z = pair_sum(pair_sum(couple_z[0::2], 1), 2)
    internal = (
        pair_sum(pair_sum(couple_x[:, 1::2], 0), 2)
        + pair_sum(pair_sum(couple_y[:, :, 1::2], 0), 1)
        + pair_sum(pair_sum(couple_z[1::2], 1), 2)
    )
    counted = pair_sum(pair_sum(pair_sum(centre_mask, 0), 1), 2)
    raw_diag = pair_sum(pair_sum(pair_sum(centre_mask * diagonal, 0), 1), 2) - 2.0 * internal
    coarse_mask = jnp.minimum(counted, 1.0)
    coarse_diag = raw_diag + (1.0 - coarse_mask)
    return ((coarse_mask, coarse_diag, coarse_x, coarse_y, coarse_z), raw_diag)


def restrict(field):
    return pair_sum(pair_sum(pair_sum(field, 1), 2), 3)


def widen(field):
    sides, planes, rows_count, cols_count = field.shape
    spread = pair_matrix(2 * cols_count).T
    along_y = jnp.matmul(field, spread, precision=lax.Precision.HIGHEST)
    grown = jnp.broadcast_to(
        along_y[:, :, None, :, None, :], (sides, planes, 2, rows_count, 2, 2 * cols_count)
    )
    return grown.reshape(sides, 2 * planes, 2 * rows_count, 2 * cols_count)


def plane_total(values):
    return jnp.sum(values, axis=(-2, -1))


def line_terms(coarse_terms, raw_diag):
    line_diag = plane_total(raw_diag) - 2.0 * (
        plane_total(coarse_terms[2]) + plane_total(coarse_terms[3])
    )
    return (line_diag, plane_total(coarse_terms[4]))


def fine_rim(field):
    return extended_2(field, (("slab", 1),), 1)


def coarse_rim(field):
    return extended_2(field, (("slab", 1),), 1)


def on_device(rhs, labels, sigma_table):
    labels_near = extended_2(labels, (("slab", 0),), 1)
    own_terms = coefficients(labels_near, sigma_table)
    source = own_terms[0] * rhs
    fine_first = start(source, own_terms)
    fine_second = smooth(fine_rim(fine_first), source, own_terms)
    fine_left = leftover(fine_rim(fine_second), source, own_terms)
    coarse_terms, raw_diag = coarsen(own_terms)
    coarse_source = restrict(fine_left)
    coarse_first = start(coarse_source, coarse_terms)
    coarse_second = smooth(coarse_rim(coarse_first), coarse_source, coarse_terms)
    coarse_left = leftover(coarse_rim(coarse_second), coarse_source, coarse_terms)
    line_diag, line_faces = line_terms(coarse_terms, raw_diag)
    planes = line_diag.shape[0]
    local_rows = plane_total(coarse_left).T
    band = jnp.stack([line_diag, line_faces[:-1]], axis=1)
    all_rows, all_band = (
        lax.all_gather(local_rows, "slab", axis=0, tiled=True),
        lax.all_gather(band, "slab", axis=0, tiled=True),
    )
    lower_band = -all_band[:, 1]
    upper_band = -jnp.concatenate([all_band[1:, 1], jnp.zeros((1,), jnp.float32)])
    line_solution = lax.linalg.tridiagonal_solve(lower_band, all_band[:, 0], upper_band, all_rows)
    own_line = lax.dynamic_slice_in_dim(line_solution, lax.axis_index("slab") * planes, planes, 0)
    coarse_fix = coarse_second + coarse_terms[0] * own_line.T[:, :, None, None]
    coarse_post = smooth(coarse_rim(coarse_fix), coarse_source, coarse_terms)
    coarse_final = smooth(coarse_rim(coarse_post), coarse_source, coarse_terms)
    fine_third = fine_second + own_terms[0] * widen(coarse_final)
    fine_fourth = smooth(fine_rim(fine_third), source, own_terms)
    return smooth(fine_rim(fine_fourth), source, own_terms)


def solution(mesh):
    placed = (P("groups", "slab", None, None), P("slab", "groups", None), P())
    return jax.shard_map(
        on_device,
        mesh=mesh,
        in_specs=placed,
        out_specs=P("groups", "slab", None, None),
        check_vma=False,
    )
```

profile of v0, /device:TPU:8, one launch (start us, length us, event | category | flops | bytes accessed | tf_op | source)
XLA Modules:
  0.0 265.4 jit_solution(3007158552615316442)
XLA Ops:
  0.0 0.9 fusion.160
  0.9 2.7 %collective-permute-start.1 = (s32[1,128,128]{2,1,0:T(8,128)S(1)}, s32[1,128,128]{2,1,0:T(8,128)S(1)}, u32[]{:S(2)}, u32[]{:S(2)}) collective-permute-start(s32[1,128,128]{2,1,0:T(8,128)S(1)} %get-tuple-element.28), channel_id=1, source_target_pairs={{1,0},{2,1},{3,2},{4,3},{5,4},{6,5},{7,6},{8,7},{9,8},{10,9},{11,1... | collective-permute-start | bytes 196616 | tf_op jit(solution)/shard_map/ppermute | solution.py:18
  3.7 1.9 collective-permute-start
  5.6 0.7 copy-done.14
  6.3 0.7 fusion.169
  7.0 0.7 copy-done.15
  7.7 0.6 dynamic-slice
  8.9 1.2 collective-permute-done
  10.5 11.2 %select_add_fusion.2 = (f32[6,130,130]{2,1,0:T(8,128)S(1)}, f32[6,130,130]{2,1,0:T(8,128)}, f32[6,130,130]{2,1,0:T(8,128)S(1)}) fusion(f32[]{:T(128)} %bitcast.6, f32[]{:T(128)} %bitcast.5, f32[]{:T(128)} %bitcast.4, f32[]{:T(128)} %bitcast.3, f32[]{:T(128)} %bitcast.2, s32[6,128,128]{2,1,0:T(8,128)S(1)} %pad_add_fusion, f32[]{:T(128)} %bitcast.16, ...), kind=kLoop, calls=%fused_computation.29 | loop fusion | flops 3244800 | bytes 1610076 | tf_op jit(solution)/shard_map/add | solution.py:30
  22.1 0.7 slice.1108
  22.8 1.7 slice_multiply_fusion.2
  24.5 0.7 slice.1110
  25.2 0.7 slice.1121
  26.2 0.9 bitcast_reduce_fusion.2
  27.3 0.6 fusion.159
  28.0 3.3 %collective-permute-start.3 = (f32[1,1,128,128]{3,2,1,0:T(8,128)}, f32[1,1,128,128]{3,2,1,0:T(8,128)}, u32[]{:S(2)}, u32[]{:S(2)}) collective-permute-start(f32[1,1,128,128]{3,2,1,0:T(8,128)} %get-tuple-element.26), channel_id=1, source_target_pairs={{1,0},{2,1},{3,2},{4,3},{5,4},{6,5},{7,6},{8,7},{9,8},{10,9},{11,1... | collective-permute-start | bytes 196616 | tf_op jit(solution)/shard_map/ppermute | solution.py:18
  31.3 1.9 collective-permute-start.2
  33.2 4.6 %slice.1109 = f32[4,128,64]{2,1,0:T(8,128)S(1)} slice(f32[4,128,129]{2,1,0:T(8,128)S(1)} %get-tuple-element.10), slice={[0:4:1], [0:128:1], [1:129:2]} | slice | bytes 262144 | tf_op jit(solution)/shard_map/slice | solution.py:108
  37.8 0.9 copy-done.6
  39.0 0.7 copy-done.7
  39.8 0.9 copy-done.8
  40.7 0.8 reduce_sum.187
  41.6 0.8 fusion.150
  43.0 0.7 fusion.165
  44.4 0.6 copy-done.10
  45.1 0.8 fusion.1
  45.9 4.5 %slice.1116 = f32[4,128,65]{2,1,0:T(8,128)S(1)} slice(f32[4,128,129]{2,1,0:T(8,128)S(1)} %get-tuple-element.10), slice={[0:4:1], [0:128:1], [0:129:2]} | slice | bytes 266240 | tf_op jit(solution)/shard_map/slice | solution.py:104
  50.5 0.7 copy.36
  51.3 0.7 copy.35
  52.2 1.2 fusion.13
  53.4 0.7 fusion.158
  54.1 4.5 %collective-permute-start.5 = (f32[1,1,128,128]{3,2,1,0:T(8,128)}, f32[1,1,128,128]{3,2,1,0:T(8,128)S(1)}, u32[]{:S(2)}, u32[]{:S(2)}) collective-permute-start(f32[1,1,128,128]{3,2,1,0:T(8,128)} %get-tuple-element.24), channel_id=1, source_target_pairs={{1,0},{2,1},{3,2},{4,3},{5,4},{6,5},{7,6},{8,7},{9,8},{10,9},{11,1... | collective-permute-start | bytes 196616 | tf_op jit(solution)/shard_map/ppermute | solution.py:18
  58.6 1.9 collective-permute-start.4
  60.9 4.4 %collective-permute-done.4 = f32[1,1,128,128]{3,2,1,0:T(8,128)S(1)} collective-permute-done((f32[1,1,128,128]{3,2,1,0:T(8,128)}, f32[1,1,128,128]{3,2,1,0:T(8,128)S(1)}, u32[]{:S(2)}, u32[]{:S(2)}) %collective-permute-start.4) | collective-permute-done | bytes 65568 | tf_op jit(solution)/shard_map/ppermute | solution.py:17
  66.0 0.6 copy-done
  66.9 15.3 %all-gather.1 = f32[16,2,2]{2,1,0:T(2,128)S(1)} all-gather(f32[1,2,2]{2,1,0:T(2,128)S(1)} %bitcast.570), channel_id=1, replica_groups=mesh['groups'=2,'slab'=16] {'slab'}, dimensions={0}, use_global_device_ids=true | all-gather | bytes 272 | tf_op jit(solution)/shard_map/all_gather | solution.py:169
  82.2 0.6 fusion.168
  83.0 0.7 fusion.167
  83.7 6.0 %collective-permute-start.7 = (f32[1,1,64,64]{3,2,1,0:T(8,128)S(1)}, f32[1,1,64,64]{3,2,1,0:T(8,128)S(1)}, u32[]{:S(2)}, u32[]{:S(2)}) collective-permute-start(f32[1,1,64,64]{3,2,1,0:T(8,128)S(1)} %get-tuple-element.40), channel_id=1, source_target_pairs={{1,0},{2,1},{3,2},{4,3},{5,4},{6,5},{7,6},{8,7},{9,8},{10,9},{11,1... | collective-permute-start | bytes 49160 | tf_op jit(solution)/shard_map/ppermute | solution.py:18
  89.7 1.9 collective-permute-start.6
  91.9 0.7 fusion.172
  92.6 0.7 fusion.170
  93.3 0.7 fusion.175
  94.0 1.8 collective-permute-done.6
  96.0 2.8 %collective-permute-start.9 = (f32[1,1,64,64]{3,2,1,0:T(8,128)S(1)}, f32[1,1,64,64]{3,2,1,0:T(8,128)S(1)}, u32[]{:S(2)}, u32[]{:S(2)}) collective-permute-start(f32[1,1,64,64]{3,2,1,0:T(8,128)S(1)} %get-tuple-element.36), channel_id=1, source_target_pairs={{1,0},{2,1},{3,2},{4,3},{5,4},{6,5},{7,6},{8,7},{9,8},{10,9},{11,1... | collective-permute-start | bytes 49160 | tf_op jit(solution)/shard_map/ppermute | solution.py:18
  98.7 2.1 collective-permute-start.8
  100.9 0.7 fusion.174
  160.8 24.9 %all-reduce.9 = f32[32]{0:T(128)S(1)} all-reduce(f32[32]{0:T(128)S(1)} %dynamic-update-slice), channel_id=2, replica_groups=mesh['groups'=2,'slab'=16] {'slab'}, use_global_device_ids=true, to_apply=%add.9 | all-reduce | flops 32 | bytes 256
  185.7 0.7 fusion.173
  186.4 0.7 fusion.171
  228.9 1.9 collective-permute-start.11
  230.8 2.4 collective-permute-start.10
  233.2 3.7 %collective-permute-done.10 = f32[1,1,64,64]{3,2,1,0:T(8,128)S(1)} collective-permute-done((f32[1,1,64,64]{3,2,1,0:T(8,128)S(1)}, f32[1,1,64,64]{3,2,1,0:T(8,128)S(1)}, u32[]{:S(2)}, u32[]{:S(2)}) %collective-permute-start.10) | collective-permute-done | bytes 16416 | tf_op jit(solution)/shard_map/ppermute | solution.py:17
  237.1 2.7 %collective-permute-start.13 = (f32[1,1,64,64]{3,2,1,0:T(8,128)S(1)}, f32[1,1,64,64]{3,2,1,0:T(8,128)S(1)}, u32[]{:S(2)}, u32[]{:S(2)}) collective-permute-start(f32[1,1,64,64]{3,2,1,0:T(8,128)S(1)} %get-tuple-element.30), channel_id=1, source_target_pairs={{1,0},{2,1},{3,2},{4,3},{5,4},{6,5},{7,6},{8,7},{9,8},{10,9},{11,1... | collective-permute-start | bytes 49160 | tf_op jit(solution)/shard_map/ppermute | solution.py:18
  239.8 1.9 collective-permute-start.12
  241.7 4.8 %collective-permute-done.12 = f32[1,1,64,64]{3,2,1,0:T(8,128)S(1)} collective-permute-done((f32[1,1,64,64]{3,2,1,0:T(8,128)S(1)}, f32[1,1,64,64]{3,2,1,0:T(8,128)S(1)}, u32[]{:S(2)}, u32[]{:S(2)}) %collective-permute-start.12) | collective-permute-done | bytes 16416 | tf_op jit(solution)/shard_map/ppermute | solution.py:17
  247.1 1.9 collective-permute-start.15
  249.0 2.4 collective-permute-start.14
  251.4 4.1 %collective-permute-done.14 = f32[1,1,128,128]{3,2,1,0:T(8,128)S(1)} collective-permute-done((f32[1,1,128,128]{3,2,1,0:T(8,128)S(1)}, f32[1,1,128,128]{3,2,1,0:T(8,128)S(1)}, u32[]{:S(2)}, u32[]{:S(2)}) %collective-permute-start.14) | collective-permute-done | bytes 65568 | tf_op jit(solution)/shard_map/ppermute | solution.py:17
  255.5 0.4 fusion.39
  255.9 1.9 collective-permute-start.17
  257.9 2.4 collective-permute-start.16
  260.3 4.1 %collective-permute-done.16 = f32[1,1,128,128]{3,2,1,0:T(8,128)S(1)} collective-permute-done((f32[1,1,128,128]{3,2,1,0:T(8,128)S(1)}, f32[1,1,128,128]{3,2,1,0:T(8,128)S(1)}, u32[]{:S(2)}, u32[]{:S(2)}) %collective-permute-start.16) | collective-permute-done | bytes 65568 | tf_op jit(solution)/shard_map/ppermute | solution.py:17
  264.4 1.1 fusion.53
  (92 shorter events, 6.6 us)
Async XLA Ops:
  0.0 10.1 %copy-start.4 = (s32[4,128,128]{2,1,0:T(8,128)S(1)}, s32[4,128,128]{2,1,0:T(8,128)}, u32[]{:S(2)}) copy-start(s32[4,128,128]{2,1,0:T(8,128)} %param.4) | copy-start | bytes 786436
  0.9 8.0 %collective-permute-start.1 = (s32[1,128,128]{2,1,0:T(8,128)S(1)}, s32[1,128,128]{2,1,0:T(8,128)S(1)}, u32[]{:S(2)}, u32[]{:S(2)}) collective-permute-start(s32[1,128,128]{2,1,0:T(8,128)S(1)} %get-tuple-element.28), channel_id=1, source_target_pairs={{1,0},{2,1},{3,2},{4,3},{5,4},{6,5},{7,6},{8,7},{9,8},{10,9},{11,1... | collective-permute-start | bytes 196616 | tf_op jit(solution)/shard_map/ppermute | solution.py:18
  3.7 6.5 %collective-permute-start = (s32[1,128,128]{2,1,0:T(8,128)S(1)}, s32[1,128,128]{2,1,0:T(8,128)S(1)}, u32[]{:S(2)}, u32[]{:S(2)}) collective-permute-start(s32[1,128,128]{2,1,0:T(8,128)S(1)} %get-tuple-element.27), channel_id=1, source_target_pairs={{0,1},{1,2},{2,3},{3,4},{4,5},{5,6},{6,7},{7,8},{8,9},{9,10},{10,1... | collective-permute-start | bytes 196616 | tf_op jit(solution)/shard_map/ppermute | solution.py:17
  5.6 0.7 copy-start.14
  7.0 0.7 copy-start.15
  26.2 1.0 copy-start.9
  28.0 24.2 %collective-permute-start.3 = (f32[1,1,128,128]{3,2,1,0:T(8,128)}, f32[1,1,128,128]{3,2,1,0:T(8,128)}, u32[]{:S(2)}, u32[]{:S(2)}) collective-permute-start(f32[1,1,128,128]{3,2,1,0:T(8,128)} %get-tuple-element.26), channel_id=1, source_target_pairs={{1,0},{2,1},{3,2},{4,3},{5,4},{6,5},{7,6},{8,7},{9,8},{10,9},{11,1... | collective-permute-start | bytes 196616 | tf_op jit(solution)/shard_map/ppermute | solution.py:18
  31.3 20.9 %collective-permute-start.2 = (f32[1,1,128,128]{3,2,1,0:T(8,128)}, f32[1,1,128,128]{3,2,1,0:T(8,128)}, u32[]{:S(2)}, u32[]{:S(2)}) collective-permute-start(f32[1,1,128,128]{3,2,1,0:T(8,128)} %get-tuple-element.25), channel_id=1, source_target_pairs={{0,1},{1,2},{2,3},{3,4},{4,5},{5,6},{6,7},{7,8},{8,9},{9,10},{10,1... | collective-permute-start | bytes 196616 | tf_op jit(solution)/shard_map/ppermute | solution.py:17
  37.8 0.9 copy-start.6
  38.8 0.9 copy-start.7
  39.8 0.9 copy-start.8
  39.8 1.7 copy-start.5
  42.6 1.1 copy-start.3
  44.2 0.8 copy-start.10
  44.2 0.9 copy-start.11
  45.9 4.6 %copy-start.13 = (f32[2,64,64]{1,2,0:T(8,128)S(1)}, f32[2,64,64]{1,2,0:T(8,128)}, u32[]{:S(2)}) copy-start(f32[2,64,64]{1,2,0:T(8,128)} %get-tuple-element.38) | copy-start | bytes 98308
  50.5 0.8 copy-start.12
  54.1 6.9 %collective-permute-start.5 = (f32[1,1,128,128]{3,2,1,0:T(8,128)}, f32[1,1,128,128]{3,2,1,0:T(8,128)S(1)}, u32[]{:S(2)}, u32[]{:S(2)}) collective-permute-start(f32[1,1,128,128]{3,2,1,0:T(8,128)} %get-tuple-element.24), channel_id=1, source_target_pairs={{1,0},{2,1},{3,2},{4,3},{5,4},{6,5},{7,6},{8,7},{9,8},{10,9},{11,1... | collective-permute-start | bytes 196616 | tf_op jit(solution)/shard_map/ppermute | solution.py:18
  58.6 6.7 %collective-permute-start.4 = (f32[1,1,128,128]{3,2,1,0:T(8,128)}, f32[1,1,128,128]{3,2,1,0:T(8,128)S(1)}, u32[]{:S(2)}, u32[]{:S(2)}) collective-permute-start(f32[1,1,128,128]{3,2,1,0:T(8,128)} %get-tuple-element.23), channel_id=1, source_target_pairs={{0,1},{1,2},{2,3},{3,4},{4,5},{5,6},{6,7},{7,8},{8,9},{9,10},{10,1... | collective-permute-start | bytes 196616 | tf_op jit(solution)/shard_map/ppermute | solution.py:17
  65.8 0.8 copy-start
  83.6 12.2 %copy-start.2 = (f32[2,64,64]{2,1,0:T(8,128)S(1)}, f32[2,64,64]{2,1,0:T(8,128)}, u32[]{:S(2)}) copy-start(f32[2,64,64]{2,1,0:T(8,128)} %copy.35) | copy-start | bytes 98308
  83.7 12.2 %copy-start.1 = (f32[2,64,64]{2,1,0:T(8,128)S(1)}, f32[2,64,64]{2,1,0:T(8,128)}, u32[]{:S(2)}) copy-start(f32[2,64,64]{2,1,0:T(8,128)} %copy.36) | copy-start | bytes 98308
  83.7 10.4 %collective-permute-start.7 = (f32[1,1,64,64]{3,2,1,0:T(8,128)S(1)}, f32[1,1,64,64]{3,2,1,0:T(8,128)S(1)}, u32[]{:S(2)}, u32[]{:S(2)}) collective-permute-start(f32[1,1,64,64]{3,2,1,0:T(8,128)S(1)} %get-tuple-element.40), channel_id=1, source_target_pairs={{1,0},{2,1},{3,2},{4,3},{5,4},{6,5},{7,6},{8,7},{9,8},{10,9},{11,1... | collective-permute-start | bytes 49160 | tf_op jit(solution)/shard_map/ppermute | solution.py:18
  89.7 6.1 %collective-permute-start.6 = (f32[1,1,64,64]{3,2,1,0:T(8,128)S(1)}, f32[1,1,64,64]{3,2,1,0:T(8,128)S(1)}, u32[]{:S(2)}, u32[]{:S(2)}) collective-permute-start(f32[1,1,64,64]{3,2,1,0:T(8,128)S(1)} %get-tuple-element.39), channel_id=1, source_target_pairs={{0,1},{1,2},{2,3},{3,4},{4,5},{5,6},{6,7},{7,8},{8,9},{9,10},{10,1... | collective-permute-start | bytes 49160 | tf_op jit(solution)/shard_map/ppermute | solution.py:17
  96.0 64.4 %collective-permute-start.9 = (f32[1,1,64,64]{3,2,1,0:T(8,128)S(1)}, f32[1,1,64,64]{3,2,1,0:T(8,128)S(1)}, u32[]{:S(2)}, u32[]{:S(2)}) collective-permute-start(f32[1,1,64,64]{3,2,1,0:T(8,128)S(1)} %get-tuple-element.36), channel_id=1, source_target_pairs={{1,0},{2,1},{3,2},{4,3},{5,4},{6,5},{7,6},{8,7},{9,8},{10,9},{11,1... | collective-permute-start | bytes 49160 | tf_op jit(solution)/shard_map/ppermute | solution.py:18
  98.7 61.6 %collective-permute-start.8 = (f32[1,1,64,64]{3,2,1,0:T(8,128)S(1)}, f32[1,1,64,64]{3,2,1,0:T(8,128)S(1)}, u32[]{:S(2)}, u32[]{:S(2)}) collective-permute-start(f32[1,1,64,64]{3,2,1,0:T(8,128)S(1)} %get-tuple-element.35), channel_id=1, source_target_pairs={{0,1},{1,2},{2,3},{3,4},{4,5},{5,6},{6,7},{7,8},{8,9},{9,10},{10,1... | collective-permute-start | bytes 49160 | tf_op jit(solution)/shard_map/ppermute | solution.py:17
  228.9 4.3 %collective-permute-start.11 = (f32[1,1,64,64]{3,2,1,0:T(8,128)S(1)}, f32[1,1,64,64]{3,2,1,0:T(8,128)S(1)}, u32[]{:S(2)}, u32[]{:S(2)}) collective-permute-start(f32[1,1,64,64]{3,2,1,0:T(8,128)S(1)} %get-tuple-element.32), channel_id=1, source_target_pairs={{1,0},{2,1},{3,2},{4,3},{5,4},{6,5},{7,6},{8,7},{9,8},{10,9},{11,1... | collective-permute-start | bytes 49160 | tf_op jit(solution)/shard_map/ppermute | solution.py:18
  230.8 6.1 %collective-permute-start.10 = (f32[1,1,64,64]{3,2,1,0:T(8,128)S(1)}, f32[1,1,64,64]{3,2,1,0:T(8,128)S(1)}, u32[]{:S(2)}, u32[]{:S(2)}) collective-permute-start(f32[1,1,64,64]{3,2,1,0:T(8,128)S(1)} %get-tuple-element.31), channel_id=1, source_target_pairs={{0,1},{1,2},{2,3},{3,4},{4,5},{5,6},{6,7},{7,8},{8,9},{9,10},{10,1... | collective-permute-start | bytes 49160 | tf_op jit(solution)/shard_map/ppermute | solution.py:17
  237.1 4.6 %collective-permute-start.13 = (f32[1,1,64,64]{3,2,1,0:T(8,128)S(1)}, f32[1,1,64,64]{3,2,1,0:T(8,128)S(1)}, u32[]{:S(2)}, u32[]{:S(2)}) collective-permute-start(f32[1,1,64,64]{3,2,1,0:T(8,128)S(1)} %get-tuple-element.30), channel_id=1, source_target_pairs={{1,0},{2,1},{3,2},{4,3},{5,4},{6,5},{7,6},{8,7},{9,8},{10,9},{11,1... | collective-permute-start | bytes 49160 | tf_op jit(solution)/shard_map/ppermute | solution.py:18
  239.8 6.8 %collective-permute-start.12 = (f32[1,1,64,64]{3,2,1,0:T(8,128)S(1)}, f32[1,1,64,64]{3,2,1,0:T(8,128)S(1)}, u32[]{:S(2)}, u32[]{:S(2)}) collective-permute-start(f32[1,1,64,64]{3,2,1,0:T(8,128)S(1)} %get-tuple-element.29), channel_id=1, source_target_pairs={{0,1},{1,2},{2,3},{3,4},{4,5},{5,6},{6,7},{7,8},{8,9},{9,10},{10,1... | collective-permute-start | bytes 49160 | tf_op jit(solution)/shard_map/ppermute | solution.py:17
  247.1 4.3 %collective-permute-start.15 = (f32[1,1,128,128]{3,2,1,0:T(8,128)S(1)}, f32[1,1,128,128]{3,2,1,0:T(8,128)S(1)}, u32[]{:S(2)}, u32[]{:S(2)}) collective-permute-start(f32[1,1,128,128]{3,2,1,0:T(8,128)S(1)} %get-tuple-element.22), channel_id=1, source_target_pairs={{1,0},{2,1},{3,2},{4,3},{5,4},{6,5},{7,6},{8,7},{9,8},{10,9},{11,1... | collective-permute-start | bytes 196616 | tf_op jit(solution)/shard_map/ppermute | solution.py:18
  249.0 6.5 %collective-permute-start.14 = (f32[1,1,128,128]{3,2,1,0:T(8,128)S(1)}, f32[1,1,128,128]{3,2,1,0:T(8,128)S(1)}, u32[]{:S(2)}, u32[]{:S(2)}) collective-permute-start(f32[1,1,128,128]{3,2,1,0:T(8,128)S(1)} %get-tuple-element.21), channel_id=1, source_target_pairs={{0,1},{1,2},{2,3},{3,4},{4,5},{5,6},{6,7},{7,8},{8,9},{9,10},{10,1... | collective-permute-start | bytes 196616 | tf_op jit(solution)/shard_map/ppermute | solution.py:17
  255.9 4.3 %collective-permute-start.17 = (f32[1,1,128,128]{3,2,1,0:T(8,128)S(1)}, f32[1,1,128,128]{3,2,1,0:T(8,128)S(1)}, u32[]{:S(2)}, u32[]{:S(2)}) collective-permute-start(f32[1,1,128,128]{3,2,1,0:T(8,128)S(1)} %get-tuple-element.20), channel_id=1, source_target_pairs={{1,0},{2,1},{3,2},{4,3},{5,4},{6,5},{7,6},{8,7},{9,8},{10,9},{11,1... | collective-permute-start | bytes 196616 | tf_op jit(solution)/shard_map/ppermute | solution.py:18
  257.9 6.5 %collective-permute-start.16 = (f32[1,1,128,128]{3,2,1,0:T(8,128)S(1)}, f32[1,1,128,128]{3,2,1,0:T(8,128)S(1)}, u32[]{:S(2)}, u32[]{:S(2)}) collective-permute-start(f32[1,1,128,128]{3,2,1,0:T(8,128)S(1)} %get-tuple-element.19), channel_id=1, source_target_pairs={{0,1},{1,2},{2,3},{3,4},{4,5},{5,6},{6,7},{7,8},{8,9},{9,10},{10,1... | collective-permute-start | bytes 196616 | tf_op jit(solution)/shard_map/ppermute | solution.py:17
where the time goes:
time: 268 us; the launch traced here: 265 us
  between operations  101 us (38%)
  starting transfers between devices  46.7 us (17%)
  blocking collectives  40.2 us (15%)
  local copies, waits for them, and re-layouts  28.7 us (11%)
  waiting for transfers between devices  24.1 us (9%)
  other arithmetic  21.2 us (8%)
  matrix products  3.07 us (1%)
    ppermute x9, starting transfers between devices, extended_2(): after = lax.ppermute(first, axis, down)  27.8 us
    unnamed x1, blocking collectives  24.9 us
    ppermute x9, waiting for transfers between devices, extended_2(): before = lax.ppermute(last, axis, up)  24.1 us
    ppermute x9, starting transfers between devices, extended_2(): before = lax.ppermute(last, axis, up)  18.9 us
    all_gather x1, blocking collectives, on_device(): lax.all_gather(band, 'slab', axis=0, tiled=True)  15.3 us
    add x1, other arithmetic, conductivity(): running + jnp.where(padded == tissue, sigma_table[tissue, column], 0.0)  11.2 us
    unnamed x39, local copies, waits for them, and re-layouts  7.66 us
    slice x8, local copies, waits for them, and re-layouts, on_device(): lax.linalg.tridiagonal_solve(lower_band, all_band[:, 0], upper_band, all_...  5.56 us
  transfers between devices with their start and end apart: 18, of which 7 were waited for; matrix products, arithmetic and copies ran while one was open for 8% of the time, Pallas kernels for 0%

commit v1 on v0

--- a/solution.py
+++ b/solution.py
@@ -5,6 +5,18 @@
 
 LABELS = 5
 OMEGA = 0.8
+
+
+def doubled_up(value, axis, dim):
+    ways, here = (lax.axis_size(axis), lax.axis_index(axis))
+    grown, reach = (value, 1)
+    while reach < ways:
+        theirs = lax.ppermute(grown, axis, [(d, d ^ reach) for d in range(ways)])
+        mine_first = jnp.concatenate([grown, theirs], axis=dim)
+        theirs_first = jnp.concatenate([theirs, grown], axis=dim)
+        grown = jnp.where(here & reach == 0, mine_first, theirs_first)
+        reach = 2 * reach
+    return grown
 
 
 def extended_2(shard, sides, width):
@@ -166,7 +178,7 @@
     band = jnp.stack([line_diag, line_faces[:-1]], axis=1)
     all_rows, all_band = (
         lax.all_gather(local_rows, "slab", axis=0, tiled=True),
-        lax.all_gather(band, "slab", axis=0, tiled=True),
+        doubled_up(band, "slab", 0),
     )
     lower_band = -all_band[:, 1]
     upper_band = -jnp.concatenate([all_band[1:, 1], jnp.zeros((1,), jnp.float32)])

time: 268 us -> 258 us (0.963)
  blocking collectives: 40.2 us -> 24.9 us
  waiting for transfers between devices: 24.1 us -> 28.9 us
    all_gather x1 -> x0, blocking collectives: 15.3 us -> none  [on_device(): lax.all_gather(band, 'slab', axis=0, tiled=True)]
    ppermute x0 -> x4, waiting for transfers between devices: none -> 6.23 us  [doubled_up(): theirs = lax.ppermute(grown, axis, [(d, d ^ reach) for d in range(ways)])]
    ppermute x9, starting transfers between devices: 27.8 us -> 25.1 us  [extended_2(): after = lax.ppermute(first, axis, down)]
    unnamed x39 -> x37, local copies, waits for them, and re-layouts: 7.66 us -> 7.56 us
  transfers between devices with their start and end apart: 18 -> 22, of which waited for: 7 -> 10; matrix products, arithmetic and copies ran while one was open for 8% -> 9% of each run, Pallas kernels for 0% -> 0%
where the time goes in v1:
time: 258 us; the launch traced here: 255 us
  between operations  101 us (39%)
  starting transfers between devices  46.7 us (18%)
  waiting for transfers between devices  28.9 us (11%)
  local copies, waits for them, and re-layouts  28.6 us (11%)
  blocking collectives  24.9 us (10%)
  other arithmetic  21.6 us (8%)
  matrix products  3.07 us (1%)
    ppermute x9, starting transfers between devices, extended_2(): after = lax.ppermute(first, axis, down)  25.1 us
    unnamed x1, blocking collectives  24.9 us
    ppermute x9, waiting for transfers between devices, extended_2(): before = lax.ppermute(last, axis, up)  22.6 us
    ppermute x9, starting transfers between devices, extended_2(): before = lax.ppermute(last, axis, up)  18.9 us
    add x1, other arithmetic, conductivity(): running + jnp.where(padded == tissue, sigma_table[tissue, column], 0.0)  11.3 us
    unnamed x37, local copies, waits for them, and re-layouts  7.56 us
    ppermute x4, waiting for transfers between devices, doubled_up(): theirs = lax.ppermute(grown, axis, [(d, d ^ reach) for d in range(ways)])  6.23 us
    slice x8, local copies, waits for them, and re-layouts, on_device(): lax.linalg.tridiagonal_solve(lower_band, all_band[:, 0], upper_band, all_...  5.72 us
  transfers between devices with their start and end apart: 22, of which 10 were waited for; matrix products, arithmetic and copies ran while one was open for 9% of the time, Pallas kernels for 0%

profile of v1, /device:TPU:8, one launch (start us, length us, event | category | flops | bytes accessed | tf_op | source)
XLA Modules:
  0.0 255.1 jit_solution(1266777987635483454)
XLA Ops:
  0.0 0.9 fusion.160
  0.9 2.7 %collective-permute-start.1 = (s32[1,128,128]{2,1,0:T(8,128)S(1)}, s32[1,128,128]{2,1,0:T(8,128)S(1)}, u32[]{:S(2)}, u32[]{:S(2)}) collective-permute-start(s32[1,128,128]{2,1,0:T(8,128)S(1)} %get-tuple-element.28), channel_id=1, source_target_pairs={{1,0},{2,1},{3,2},{4,3},{5,4},{6,5},{7,6},{8,7},{9,8},{10,9},{11,1... | collective-permute-start | bytes 196616 | tf_op jit(solution)/shard_map/ppermute | solution.py:30
  3.7 1.9 collective-permute-start
  5.6 0.7 copy-done.14
  6.3 0.7 fusion.167
  7.0 0.6 copy-done.15
  7.7 0.6 dynamic-slice
  9.0 1.1 collective-permute-done
  10.5 11.3 %select_add_fusion.2 = (f32[6,130,130]{2,1,0:T(8,128)S(1)}, f32[6,130,130]{2,1,0:T(8,128)}, f32[6,130,130]{2,1,0:T(8,128)S(1)}) fusion(f32[]{:T(128)} %bitcast.6, f32[]{:T(128)} %bitcast.5, f32[]{:T(128)} %bitcast.4, f32[]{:T(128)} %bitcast.3, f32[]{:T(128)} %bitcast.2, s32[6,128,128]{2,1,0:T(8,128)S(1)} %pad_add_fusion, f32[]{:T(128)} %bitcast.16, ...), kind=kLoop, calls=%fused_computation.29 | loop fusion | flops 3244800 | bytes 1610076 | tf_op jit(solution)/shard_map/add | solution.py:42
  22.1 0.7 slice.1108
  22.8 1.7 slice_multiply_fusion.2
  24.6 0.7 slice.1110
  25.2 0.7 slice.1121
  26.3 0.9 bitcast_reduce_fusion.2
  27.4 0.7 fusion.159
  28.1 3.4 %collective-permute-start.3 = (f32[1,1,128,128]{3,2,1,0:T(8,128)}, f32[1,1,128,128]{3,2,1,0:T(8,128)}, u32[]{:S(2)}, u32[]{:S(2)}) collective-permute-start(f32[1,1,128,128]{3,2,1,0:T(8,128)} %get-tuple-element.26), channel_id=1, source_target_pairs={{1,0},{2,1},{3,2},{4,3},{5,4},{6,5},{7,6},{8,7},{9,8},{10,9},{11,1... | collective-permute-start | bytes 196616 | tf_op jit(solution)/shard_map/ppermute | solution.py:30
  31.5 1.9 collective-permute-start.2
  33.4 4.6 %slice.1109 = f32[4,128,64]{2,1,0:T(8,128)S(1)} slice(f32[4,128,129]{2,1,0:T(8,128)S(1)} %get-tuple-element.10), slice={[0:4:1], [0:128:1], [1:129:2]} | slice | bytes 262144 | tf_op jit(solution)/shard_map/slice | solution.py:120
  38.0 0.9 copy-done.6
  39.2 0.7 copy-done.7
  40.0 0.9 copy-done.8
  40.9 0.8 reduce_sum.187
  41.8 0.8 fusion.150
  43.2 0.7 fusion.165
  44.6 0.6 copy-done.10
  45.3 0.8 fusion.1
  46.1 4.5 %slice.1116 = f32[4,128,65]{2,1,0:T(8,128)S(1)} slice(f32[4,128,129]{2,1,0:T(8,128)S(1)} %get-tuple-element.10), slice={[0:4:1], [0:128:1], [0:129:2]} | slice | bytes 266240 | tf_op jit(solution)/shard_map/slice | solution.py:116
  50.7 0.7 copy.21
  51.5 0.7 copy.20
  52.4 1.2 fusion.13
  53.6 0.7 fusion.158
  54.3 4.5 %collective-permute-start.5 = (f32[1,1,128,128]{3,2,1,0:T(8,128)}, f32[1,1,128,128]{3,2,1,0:T(8,128)S(1)}, u32[]{:S(2)}, u32[]{:S(2)}) collective-permute-start(f32[1,1,128,128]{3,2,1,0:T(8,128)} %get-tuple-element.24), channel_id=1, source_target_pairs={{1,0},{2,1},{3,2},{4,3},{5,4},{6,5},{7,6},{8,7},{9,8},{10,9},{11,1... | collective-permute-start | bytes 196616 | tf_op jit(solution)/shard_map/ppermute | solution.py:30
  58.8 1.9 collective-permute-start.4
  61.1 4.4 %collective-permute-done.4 = f32[1,1,128,128]{3,2,1,0:T(8,128)S(1)} collective-permute-done((f32[1,1,128,128]{3,2,1,0:T(8,128)}, f32[1,1,128,128]{3,2,1,0:T(8,128)S(1)}, u32[]{:S(2)}, u32[]{:S(2)}) %collective-permute-start.4) | collective-permute-done | bytes 65568 | tf_op jit(solution)/shard_map/ppermute | solution.py:29
  67.1 1.1 collective-permute-done.10
  68.3 3.6 %collective-permute-done.11 = f32[4,2]{0,1:T(2,128)S(1)} collective-permute-done((f32[4,2]{0,1:T(2,128)S(1)}, f32[4,2]{0,1:T(2,128)S(1)}, u32[]{:S(2)}, u32[]{:S(2)}) %collective-permute-start.11) | collective-permute-done | bytes 64 | tf_op jit(solution)/shard_map/ppermute | solution.py:14
  72.0 2.0 collective-permute-start.7
  74.0 1.6 collective-permute-done.12
  75.6 2.6 %collective-permute-start.13 = (f32[16,2]{0,1:T(2,128)S(1)}, f32[16,2]{0,1:T(2,128)S(1)}, u32[]{:S(2)}, u32[]{:S(2)}) collective-permute-start(f32[16,2]{0,1:T(2,128)S(1)} %maximum_select_fusion.2), channel_id=1, source_target_pairs={{0,8},{1,9},{2,10},{3,11},{4,12},{5,13},{6,14},{7,15},{8,0},{9,1},... | collective-permute-start | bytes 392 | tf_op jit(solution)/shard_map/ppermute | solution.py:14
  78.2 1.9 collective-permute-start.6
  80.2 0.7 fusion.169
  81.0 0.7 fusion.168
  81.8 0.7 fusion.172
  82.5 0.7 fusion.170
  83.3 0.7 fusion.175
  84.5 4.2 %collective-permute-start.9 = (f32[1,1,64,64]{3,2,1,0:T(8,128)S(1)}, f32[1,1,64,64]{3,2,1,0:T(8,128)S(1)}, u32[]{:S(2)}, u32[]{:S(2)}) collective-permute-start(f32[1,1,64,64]{3,2,1,0:T(8,128)S(1)} %get-tuple-element.36), channel_id=1, source_target_pairs={{1,0},{2,1},{3,2},{4,3},{5,4},{6,5},{7,6},{8,7},{9,8},{10,9},{11,1... | collective-permute-start | bytes 49160 | tf_op jit(solution)/shard_map/ppermute | solution.py:30
  88.7 2.1 collective-permute-start.8
  90.8 0.7 fusion.174
  150.8 24.9 %all-reduce.9 = f32[32]{0:T(128)S(1)} all-reduce(f32[32]{0:T(128)S(1)} %dynamic-update-slice), channel_id=2, replica_groups=mesh['groups'=2,'slab'=16] {'slab'}, use_global_device_ids=true, to_apply=%add.9 | all-reduce | flops 32 | bytes 256
  175.7 0.7 fusion.173
  176.4 0.7 fusion.171
  218.7 1.9 collective-permute-start.15
  220.6 2.4 collective-permute-start.14
  223.1 3.7 %collective-permute-done.14 = f32[1,1,64,64]{3,2,1,0:T(8,128)S(1)} collective-permute-done((f32[1,1,64,64]{3,2,1,0:T(8,128)S(1)}, f32[1,1,64,64]{3,2,1,0:T(8,128)S(1)}, u32[]{:S(2)}, u32[]{:S(2)}) %collective-permute-start.14) | collective-permute-done | bytes 16416 | tf_op jit(solution)/shard_map/ppermute | solution.py:29
  226.9 2.4 collective-permute-start.17
  229.4 1.9 collective-permute-start.16
  231.3 4.9 %collective-permute-done.16 = f32[1,1,64,64]{3,2,1,0:T(8,128)S(1)} collective-permute-done((f32[1,1,64,64]{3,2,1,0:T(8,128)S(1)}, f32[1,1,64,64]{3,2,1,0:T(8,128)S(1)}, u32[]{:S(2)}, u32[]{:S(2)}) %collective-permute-start.16) | collective-permute-done | bytes 16416 | tf_op jit(solution)/shard_map/ppermute | solution.py:29
  236.7 1.9 collective-permute-start.19
  238.7 2.4 collective-permute-start.18
  241.1 4.1 %collective-permute-done.18 = f32[1,1,128,128]{3,2,1,0:T(8,128)S(1)} collective-permute-done((f32[1,1,128,128]{3,2,1,0:T(8,128)S(1)}, f32[1,1,128,128]{3,2,1,0:T(8,128)S(1)}, u32[]{:S(2)}, u32[]{:S(2)}) %collective-permute-start.18) | collective-permute-done | bytes 65568 | tf_op jit(solution)/shard_map/ppermute | solution.py:29
  245.6 1.9 collective-permute-start.21
  247.5 2.4 collective-permute-start.20
  250.0 4.1 %collective-permute-done.20 = f32[1,1,128,128]{3,2,1,0:T(8,128)S(1)} collective-permute-done((f32[1,1,128,128]{3,2,1,0:T(8,128)S(1)}, f32[1,1,128,128]{3,2,1,0:T(8,128)S(1)}, u32[]{:S(2)}, u32[]{:S(2)}) %collective-permute-start.20) | collective-permute-done | bytes 65568 | tf_op jit(solution)/shard_map/ppermute | solution.py:29
  254.0 1.1 fusion.53
  (99 shorter events, 8.1 us)
Async XLA Ops:
  0.0 10.1 %copy-start.4 = (s32[4,128,128]{2,1,0:T(8,128)S(1)}, s32[4,128,128]{2,1,0:T(8,128)}, u32[]{:S(2)}) copy-start(s32[4,128,128]{2,1,0:T(8,128)} %param.4) | copy-start | bytes 786436
  0.9 8.1 %collective-permute-start.1 = (s32[1,128,128]{2,1,0:T(8,128)S(1)}, s32[1,128,128]{2,1,0:T(8,128)S(1)}, u32[]{:S(2)}, u32[]{:S(2)}) collective-permute-start(s32[1,128,128]{2,1,0:T(8,128)S(1)} %get-tuple-element.28), channel_id=1, source_target_pairs={{1,0},{2,1},{3,2},{4,3},{5,4},{6,5},{7,6},{8,7},{9,8},{10,9},{11,1... | collective-permute-start | bytes 196616 | tf_op jit(solution)/shard_map/ppermute | solution.py:30
  3.7 6.5 %collective-permute-start = (s32[1,128,128]{2,1,0:T(8,128)S(1)}, s32[1,128,128]{2,1,0:T(8,128)S(1)}, u32[]{:S(2)}, u32[]{:S(2)}) collective-permute-start(s32[1,128,128]{2,1,0:T(8,128)S(1)} %get-tuple-element.27), channel_id=1, source_target_pairs={{0,1},{1,2},{2,3},{3,4},{4,5},{5,6},{6,7},{7,8},{8,9},{9,10},{10,1... | collective-permute-start | bytes 196616 | tf_op jit(solution)/shard_map/ppermute | solution.py:29
  5.6 0.7 copy-start.14
  7.0 0.7 copy-start.15
  26.3 1.0 copy-start.9
  28.1 24.3 %collective-permute-start.3 = (f32[1,1,128,128]{3,2,1,0:T(8,128)}, f32[1,1,128,128]{3,2,1,0:T(8,128)}, u32[]{:S(2)}, u32[]{:S(2)}) collective-permute-start(f32[1,1,128,128]{3,2,1,0:T(8,128)} %get-tuple-element.26), channel_id=1, source_target_pairs={{1,0},{2,1},{3,2},{4,3},{5,4},{6,5},{7,6},{8,7},{9,8},{10,9},{11,1... | collective-permute-start | bytes 196616 | tf_op jit(solution)/shard_map/ppermute | solution.py:30
  31.5 20.9 %collective-permute-start.2 = (f32[1,1,128,128]{3,2,1,0:T(8,128)}, f32[1,1,128,128]{3,2,1,0:T(8,128)}, u32[]{:S(2)}, u32[]{:S(2)}) collective-permute-start(f32[1,1,128,128]{3,2,1,0:T(8,128)} %get-tuple-element.25), channel_id=1, source_target_pairs={{0,1},{1,2},{2,3},{3,4},{4,5},{5,6},{6,7},{7,8},{8,9},{9,10},{10,1... | collective-permute-start | bytes 196616 | tf_op jit(solution)/shard_map/ppermute | solution.py:29
  38.0 0.9 copy-start.6
  39.0 0.9 copy-start.7
  40.0 0.9 copy-start.8
  40.0 1.7 copy-start.5
  42.8 1.1 copy-start.3
  44.4 0.8 copy-start.10
  44.4 0.9 copy-start.11
  46.1 4.6 %copy-start.13 = (f32[2,64,64]{1,2,0:T(8,128)S(1)}, f32[2,64,64]{1,2,0:T(8,128)}, u32[]{:S(2)}) copy-start(f32[2,64,64]{1,2,0:T(8,128)} %get-tuple-element.38) | copy-start | bytes 98308
  50.7 0.8 copy-start.12
  54.3 6.9 %collective-permute-start.5 = (f32[1,1,128,128]{3,2,1,0:T(8,128)}, f32[1,1,128,128]{3,2,1,0:T(8,128)S(1)}, u32[]{:S(2)}, u32[]{:S(2)}) collective-permute-start(f32[1,1,128,128]{3,2,1,0:T(8,128)} %get-tuple-element.24), channel_id=1, source_target_pairs={{1,0},{2,1},{3,2},{4,3},{5,4},{6,5},{7,6},{8,7},{9,8},{10,9},{11,1... | collective-permute-start | bytes 196616 | tf_op jit(solution)/shard_map/ppermute | solution.py:30
  58.8 6.7 %collective-permute-start.4 = (f32[1,1,128,128]{3,2,1,0:T(8,128)}, f32[1,1,128,128]{3,2,1,0:T(8,128)S(1)}, u32[]{:S(2)}, u32[]{:S(2)}) collective-permute-start(f32[1,1,128,128]{3,2,1,0:T(8,128)} %get-tuple-element.23), channel_id=1, source_target_pairs={{0,1},{1,2},{2,3},{3,4},{4,5},{5,6},{6,7},{7,8},{8,9},{9,10},{10,1... | collective-permute-start | bytes 196616 | tf_op jit(solution)/shard_map/ppermute | solution.py:29
  66.0 0.8 copy-start
  67.0 17.3 %copy-start.2 = (f32[2,64,64]{2,1,0:T(8,128)S(1)}, f32[2,64,64]{2,1,0:T(8,128)}, u32[]{:S(2)}) copy-start(f32[2,64,64]{2,1,0:T(8,128)} %copy.20) | copy-start | bytes 98308
  67.0 17.3 %copy-start.1 = (f32[2,64,64]{2,1,0:T(8,128)S(1)}, f32[2,64,64]{2,1,0:T(8,128)}, u32[]{:S(2)}) copy-start(f32[2,64,64]{2,1,0:T(8,128)} %copy.21) | copy-start | bytes 98308
  67.0 1.2 collective-permute-start.10
  68.3 3.6 %collective-permute-start.11 = (f32[4,2]{0,1:T(2,128)S(1)}, f32[4,2]{0,1:T(2,128)S(1)}, u32[]{:S(2)}, u32[]{:S(2)}) collective-permute-start(f32[4,2]{0,1:T(2,128)S(1)} %maximum_select_fusion), channel_id=1, source_target_pairs={{0,2},{1,3},{2,0},{3,1},{4,6},{5,7},{6,4},{7,5},{8,10},{9,11},{10,... | collective-permute-start | bytes 104 | tf_op jit(solution)/shard_map/ppermute | solution.py:14
  72.0 3.6 %collective-permute-start.12 = (f32[8,2]{0,1:T(2,128)S(1)}, f32[8,2]{0,1:T(2,128)S(1)}, u32[]{:S(2)}, u32[]{:S(2)}) collective-permute-start(f32[8,2]{0,1:T(2,128)S(1)} %maximum_select_fusion.1), channel_id=1, source_target_pairs={{0,4},{1,5},{2,6},{3,7},{4,0},{5,1},{6,2},{7,3},{8,12},{9,13},{10,... | collective-permute-start | bytes 200 | tf_op jit(solution)/shard_map/ppermute | solution.py:14
  72.0 12.0 %collective-permute-start.7 = (f32[1,1,64,64]{3,2,1,0:T(8,128)S(1)}, f32[1,1,64,64]{3,2,1,0:T(8,128)S(1)}, u32[]{:S(2)}, u32[]{:S(2)}) collective-permute-start(f32[1,1,64,64]{3,2,1,0:T(8,128)S(1)} %get-tuple-element.40), channel_id=1, source_target_pairs={{1,0},{2,1},{3,2},{4,3},{5,4},{6,5},{7,6},{8,7},{9,8},{10,9},{11,1... | collective-permute-start | bytes 49160 | tf_op jit(solution)/shard_map/ppermute | solution.py:30
  75.6 4.5 %collective-permute-start.13 = (f32[16,2]{0,1:T(2,128)S(1)}, f32[16,2]{0,1:T(2,128)S(1)}, u32[]{:S(2)}, u32[]{:S(2)}) collective-permute-start(f32[16,2]{0,1:T(2,128)S(1)} %maximum_select_fusion.2), channel_id=1, source_target_pairs={{0,8},{1,9},{2,10},{3,11},{4,12},{5,13},{6,14},{7,15},{8,0},{9,1},... | collective-permute-start | bytes 392 | tf_op jit(solution)/shard_map/ppermute | solution.py:14
  78.2 6.1 %collective-permute-start.6 = (f32[1,1,64,64]{3,2,1,0:T(8,128)S(1)}, f32[1,1,64,64]{3,2,1,0:T(8,128)S(1)}, u32[]{:S(2)}, u32[]{:S(2)}) collective-permute-start(f32[1,1,64,64]{3,2,1,0:T(8,128)S(1)} %get-tuple-element.39), channel_id=1, source_target_pairs={{0,1},{1,2},{2,3},{3,4},{4,5},{5,6},{6,7},{7,8},{8,9},{9,10},{10,1... | collective-permute-start | bytes 49160 | tf_op jit(solution)/shard_map/ppermute | solution.py:29
  84.5 65.8 %collective-permute-start.9 = (f32[1,1,64,64]{3,2,1,0:T(8,128)S(1)}, f32[1,1,64,64]{3,2,1,0:T(8,128)S(1)}, u32[]{:S(2)}, u32[]{:S(2)}) collective-permute-start(f32[1,1,64,64]{3,2,1,0:T(8,128)S(1)} %get-tuple-element.36), channel_id=1, source_target_pairs={{1,0},{2,1},{3,2},{4,3},{5,4},{6,5},{7,6},{8,7},{9,8},{10,9},{11,1... | collective-permute-start | bytes 49160 | tf_op jit(solution)/shard_map/ppermute | solution.py:30
  88.7 61.6 %collective-permute-start.8 = (f32[1,1,64,64]{3,2,1,0:T(8,128)S(1)}, f32[1,1,64,64]{3,2,1,0:T(8,128)S(1)}, u32[]{:S(2)}, u32[]{:S(2)}) collective-permute-start(f32[1,1,64,64]{3,2,1,0:T(8,128)S(1)} %get-tuple-element.35), channel_id=1, source_target_pairs={{0,1},{1,2},{2,3},{3,4},{4,5},{5,6},{6,7},{7,8},{8,9},{9,10},{10,1... | collective-permute-start | bytes 49160 | tf_op jit(solution)/shard_map/ppermute | solution.py:29
  218.7 4.3 %collective-permute-start.15 = (f32[1,1,64,64]{3,2,1,0:T(8,128)S(1)}, f32[1,1,64,64]{3,2,1,0:T(8,128)S(1)}, u32[]{:S(2)}, u32[]{:S(2)}) collective-permute-start(f32[1,1,64,64]{3,2,1,0:T(8,128)S(1)} %get-tuple-element.32), channel_id=1, source_target_pairs={{1,0},{2,1},{3,2},{4,3},{5,4},{6,5},{7,6},{8,7},{9,8},{10,9},{11,1... | collective-permute-start | bytes 49160 | tf_op jit(solution)/shard_map/ppermute | solution.py:30
  220.6 6.1 %collective-permute-start.14 = (f32[1,1,64,64]{3,2,1,0:T(8,128)S(1)}, f32[1,1,64,64]{3,2,1,0:T(8,128)S(1)}, u32[]{:S(2)}, u32[]{:S(2)}) collective-permute-start(f32[1,1,64,64]{3,2,1,0:T(8,128)S(1)} %get-tuple-element.31), channel_id=1, source_target_pairs={{0,1},{1,2},{2,3},{3,4},{4,5},{5,6},{6,7},{7,8},{8,9},{9,10},{10,1... | collective-permute-start | bytes 49160 | tf_op jit(solution)/shard_map/ppermute | solution.py:29
  226.9 4.4 %collective-permute-start.17 = (f32[1,1,64,64]{3,2,1,0:T(8,128)S(1)}, f32[1,1,64,64]{3,2,1,0:T(8,128)S(1)}, u32[]{:S(2)}, u32[]{:S(2)}) collective-permute-start(f32[1,1,64,64]{3,2,1,0:T(8,128)S(1)} %get-tuple-element.30), channel_id=1, source_target_pairs={{1,0},{2,1},{3,2},{4,3},{5,4},{6,5},{7,6},{8,7},{9,8},{10,9},{11,1... | collective-permute-start | bytes 49160 | tf_op jit(solution)/shard_map/ppermute | solution.py:30
  229.4 6.9 %collective-permute-start.16 = (f32[1,1,64,64]{3,2,1,0:T(8,128)S(1)}, f32[1,1,64,64]{3,2,1,0:T(8,128)S(1)}, u32[]{:S(2)}, u32[]{:S(2)}) collective-permute-start(f32[1,1,64,64]{3,2,1,0:T(8,128)S(1)} %get-tuple-element.29), channel_id=1, source_target_pairs={{0,1},{1,2},{2,3},{3,4},{4,5},{5,6},{6,7},{7,8},{8,9},{9,10},{10,1... | collective-permute-start | bytes 49160 | tf_op jit(solution)/shard_map/ppermute | solution.py:29
  236.7 4.3 %collective-permute-start.19 = (f32[1,1,128,128]{3,2,1,0:T(8,128)S(1)}, f32[1,1,128,128]{3,2,1,0:T(8,128)S(1)}, u32[]{:S(2)}, u32[]{:S(2)}) collective-permute-start(f32[1,1,128,128]{3,2,1,0:T(8,128)S(1)} %get-tuple-element.22), channel_id=1, source_target_pairs={{1,0},{2,1},{3,2},{4,3},{5,4},{6,5},{7,6},{8,7},{9,8},{10,9},{11,1... | collective-permute-start | bytes 196616 | tf_op jit(solution)/shard_map/ppermute | solution.py:30
  238.7 6.5 %collective-permute-start.18 = (f32[1,1,128,128]{3,2,1,0:T(8,128)S(1)}, f32[1,1,128,128]{3,2,1,0:T(8,128)S(1)}, u32[]{:S(2)}, u32[]{:S(2)}) collective-permute-start(f32[1,1,128,128]{3,2,1,0:T(8,128)S(1)} %get-tuple-element.21), channel_id=1, source_target_pairs={{0,1},{1,2},{2,3},{3,4},{4,5},{5,6},{6,7},{7,8},{8,9},{9,10},{10,1... | collective-permute-start | bytes 196616 | tf_op jit(solution)/shard_map/ppermute | solution.py:29
  245.6 4.3 %collective-permute-start.21 = (f32[1,1,128,128]{3,2,1,0:T(8,128)S(1)}, f32[1,1,128,128]{3,2,1,0:T(8,128)S(1)}, u32[]{:S(2)}, u32[]{:S(2)}) collective-permute-start(f32[1,1,128,128]{3,2,1,0:T(8,128)S(1)} %get-tuple-element.20), channel_id=1, source_target_pairs={{1,0},{2,1},{3,2},{4,3},{5,4},{6,5},{7,6},{8,7},{9,8},{10,9},{11,1... | collective-permute-start | bytes 196616 | tf_op jit(solution)/shard_map/ppermute | solution.py:30
  247.5 6.5 %collective-permute-start.20 = (f32[1,1,128,128]{3,2,1,0:T(8,128)S(1)}, f32[1,1,128,128]{3,2,1,0:T(8,128)S(1)}, u32[]{:S(2)}, u32[]{:S(2)}) collective-permute-start(f32[1,1,128,128]{3,2,1,0:T(8,128)S(1)} %get-tuple-element.19), channel_id=1, source_target_pairs={{0,1},{1,2},{2,3},{3,4},{4,5},{5,6},{6,7},{7,8},{8,9},{9,10},{10,1... | collective-permute-start | bytes 196616 | tf_op jit(solution)/shard_map/ppermute | solution.py:29
